TPU v7x, 512 devices: a whole 4x4x16 slice. The times are simulated.
512 devices in a mesh: lat: 4 (over y_hi, core), lon: 128 (over x, z, y_lo).
Axes of the slice: x: 4, y: 4 (y_hi: 2, y_lo: 2; y = y_hi * 2 + y_lo), z: 16, core: 2. Of those that a mesh axis runs over, the one named last changes fastest.
Arguments:
- features: bfloat16 [128, 1024, 1024], P('lat', 'lon'), may hold values from -18 to 18
- depth_kernel: bfloat16 [7, 7, 1024], replicated, may hold values from -0.875 to 0.875
- depth_bias: float32 [1024], replicated, may hold values from -3 to 3
- norm_gain: float32 [1024], replicated, may hold values from 0.1 to 1.9
- norm_bias: float32 [1024], replicated, may hold values from -3 to 3
- up_weight: bfloat16 [1024, 4096], P('lon', 'lat'), may hold values from -0.1875 to 0.1875
- up_bias: float32 [4096], P('lat'), may hold values from -3 to 3
- down_weight: bfloat16 [1024, 4096], P('lon', 'lat'), may hold values from -0.09375 to 0.09375
- down_bias: float32 [1024], replicated, may hold values from -3 to 3
- layer_scale: float32 [1024], replicated, may hold values from 0.3 to 2
Outputs:
- updated: bfloat16 [128, 1024, 1024], P('lat', 'lon')
All inputs are finite; a program needn't handle non-finite values.
Results may differ from a plain program's by a relative error of at most 0.0085.
Values may be sent and summed in bfloat16 or wider, within the bound.
A program may use at most 64 MiB of HBM per device.

v0:
```python
import jax
import jax.numpy as jnp
from jax import lax
from jax.sharding import PartitionSpec as P


def with_halo(block, sides, width, periodic):
    for axis, dim in sides:
        count = lax.axis_size(axis)
        forward = [(i, i + 1) for i in range(count - 1)]
        if periodic:
            forward.append((count - 1, 0))
        backward = [(target, source) for source, target in forward]
        low = lax.ppermute(
            lax.slice_in_dim(block, block.shape[dim] - width, None, axis=dim), axis, forward
        )
        high = lax.ppermute(lax.slice_in_dim(block, 0, width, axis=dim), axis, backward)
        block = jnp.concatenate([low, block, high], axis=dim)
    return block


def staged_gather(shard):
    count = lax.axis_size("lon")
    n_x, n_y = (4, 2)
    n_z = count // (n_x * n_y)
    index = lambda x, z, y: (x * n_z + z) * n_y + y
    by_y = [[index(x, z, y) for y in range(n_y)] for x in range(n_x) for z in range(n_z)]
    by_x = [[index(x, z, y) for x in range(n_x)] for z in range(n_z) for y in range(n_y)]
    by_z = [[index(x, z, y) for z in range(n_z)] for x in range(n_x) for y in range(n_y)]
    part = lax.all_gather(shard, "lon", axis=0, axis_index_groups=by_y)
    part = lax.all_gather(part, "lon", axis=0, axis_index_groups=by_x)
    part = lax.all_gather(part, "lon", axis=0, axis_index_groups=by_z)
    part = jnp.swapaxes(part, 0, 1)
    return part.reshape((count * shard.shape[0],) + shard.shape[1:])


def local(
    features,
    depth_kernel,
    depth_bias,
    norm_gain,
    norm_bias,
    up_weight,
    up_bias,
    down_weight,
    down_bias,
    layer_scale,
):
    row_count, col_count, chan_count = features.shape
    circled = with_halo(features, (("lon", 1),), 3, True)
    padded = with_halo(circled, (("lat", 0),), 3, False)
    kernel = depth_kernel.astype(jnp.float32)
    total = jnp.zeros((row_count, col_count, chan_count), jnp.float32) + depth_bias
    for row_off in range(7):
        for col_off in range(7):
            window = padded[row_off : row_off + row_count, col_off : col_off + col_count].astype(
                jnp.float32
            )
            total = total + window * kernel[row_off, col_off]
    centre = jnp.mean(total, axis=-1, keepdims=True)
    spread = jnp.mean((total - centre) ** 2, axis=-1, keepdims=True)
    normed = ((total - centre) * lax.rsqrt(spread + 1e-06) * norm_gain + norm_bias).astype(
        jnp.bfloat16
    )
    normed = normed.reshape(row_count * col_count, chan_count)
    gathered = lax.all_gather(normed, "lat", axis=0, tiled=True)
    pre = jnp.dot(gathered, staged_gather(up_weight), preferred_element_type=jnp.float32) + up_bias
    hidden = jax.nn.gelu(pre, approximate=False).astype(jnp.bfloat16)
    partial_out = lax.dot_general(
        hidden,
        staged_gather(down_weight),
        (((1,), (1,)), ((), ())),
        preferred_element_type=jnp.float32,
    )
    branch = lax.psum_scatter(
        partial_out.astype(jnp.bfloat16), "lat", scatter_dimension=0, tiled=True
    ).astype(jnp.float32)
    branch = branch.reshape(row_count, col_count, chan_count)
    updated = features.astype(jnp.float32) + layer_scale * (branch + down_bias)
    return updated.astype(jnp.bfloat16)


def solution(mesh):
    placed = (
        P("lat", "lon", None),
        P(),
        P(),
        P(),
        P(),
        P("lon", "lat"),
        P("lat"),
        P("lon", "lat"),
        P(),
        P(),
    )
    return jax.shard_map(
        local, mesh=mesh, in_specs=placed, out_specs=P("lat", "lon", None), check_vma=False
    )
```

profile of v0, /device:TPU:1, one launch (start us, length us, event | category | flops | bytes accessed | tf_op | source)
XLA Modules:
  0.0 285.6 jit_solution(13402974047549205243)
XLA Ops:
  6.5 4.3 %all-gather = bf16[16,1024]{1,0:T(8,128)(2,1)S(1)} all-gather(bf16[8,1024]{1,0:T(8,128)(2,1)} %param.15), channel_id=2, replica_groups={{0,1},{2,3},{4,5},{6,7},{8,9},{10,11},{12,13},{14,15},{16,17},{18,19},{..., dimensions={0}, use_global_device_ids=true | all-gather | bytes 49152 | tf_op jit(solution)/shard_map/all_gather | solution.py:30
  10.8 10.3 %all-gather.1 = bf16[8,8,1024]{2,1,0:T(8,128)(2,1)} all-gather(bf16[2,8,1024]{2,1,0:T(8,128)(2,1)S(1)} %bitcast.75), channel_id=3, replica_groups={{0,32,64,96},{1,33,65,97},{2,34,66,98},{3,35,67,99},{4,36,68,100},{5,37..., dimensions={0}, use_global_device_ids=true | all-gather | bytes 163840 | tf_op jit(solution)/shard_map/all_gather | solution.py:31
  21.1 0.0 all-gather.12.cloned.1.call-update
  21.2 0.0 all-gather.14.cloned.1.call-start
  21.2 1.4 fusion.79
  22.7 3.2 %collective-permute-start = (bf16[32,3,1024]{2,1,0:T(4,128)(2,1)S(1)}, bf16[32,3,1024]{2,1,0:T(4,128)(2,1)S(1)}, u32[]{:S(2)}, u32[]{:S(2)}) collective-permute-start(bf16[32,3,1024]{2,1,0:T(4,128)(2,1)S(1)} %get-tuple-element.11), channel_id=1, source_target_pairs={{0,1},{1,2},{2,3},{3,4},{4,5},{5,6},{6,7},{7,8},{8,9},{9,10},{10,1... | collective-permute-start | bytes 589832 | tf_op jit(solution)/shard_map/ppermute | solution.py:14
  25.9 12.7 %collective-permute-start.1 = (bf16[32,3,1024]{2,1,0:T(4,128)(2,1)S(1)}, bf16[32,3,1024]{2,1,0:T(4,128)(2,1)S(1)}, u32[]{:S(2)}, u32[]{:S(2)}) collective-permute-start(bf16[32,3,1024]{2,1,0:T(4,128)(2,1)S(1)} %get-tuple-element.12), channel_id=1, source_target_pairs={{1,0},{2,1},{3,2},{4,3},{5,4},{6,5},{7,6},{8,7},{9,8},{10,9},{11,1... | collective-permute-start | bytes 589832 | tf_op jit(solution)/shard_map/ppermute | solution.py:17
  38.6 4.0 %all-gather.3 = bf16[16,1024]{1,0:T(8,128)(2,1)S(1)} all-gather(bf16[8,1024]{1,0:T(8,128)(2,1)} %param.17), channel_id=5, replica_groups={{0,1},{2,3},{4,5},{6,7},{8,9},{10,11},{12,13},{14,15},{16,17},{18,19},{..., dimensions={0}, use_global_device_ids=true | all-gather | bytes 49152 | tf_op jit(solution)/shard_map/all_gather | solution.py:30
  42.6 9.8 %all-gather.4 = bf16[8,8,1024]{2,1,0:T(8,128)(2,1)} all-gather(bf16[2,8,1024]{2,1,0:T(8,128)(2,1)S(1)} %bitcast.76), channel_id=6, replica_groups={{0,32,64,96},{1,33,65,97},{2,34,66,98},{3,35,67,99},{4,36,68,100},{5,37..., dimensions={0}, use_global_device_ids=true | all-gather | bytes 163840 | tf_op jit(solution)/shard_map/all_gather | solution.py:31
  52.5 0.0 all-gather.14.cloned.1.call-update
  52.5 0.0 all-gather.10.cloned.1.call-start
  52.5 1.2 fusion.80
  53.8 0.1 fusion.81
  53.9 0.1 pad_maximum_fusion.4
  54.0 12.9 %collective-permute-start.2 = (bf16[3,14,1024]{2,1,0:T(8,128)(2,1)S(1)}, bf16[3,14,1024]{2,1,0:T(8,128)(2,1)S(1)}, u32[]{:S(2)}, u32[]{:S(2)}) collective-permute-start(bf16[3,14,1024]{2,1,0:T(8,128)(2,1)S(1)} %get-tuple-element.9), channel_id=1, source_target_pairs={{0,128},{128,256},{256,384},{1,129},{129,257},{257,385},{2,130},{1... | collective-permute-start | bytes 258056 | tf_op jit(solution)/shard_map/ppermute | solution.py:14
  66.9 1.9 collective-permute-start.3
  68.8 0.2 constant_dynamic-update-slice_fusion
  69.0 5.4 %collective-permute-done.3 = bf16[3,14,1024]{2,1,0:T(8,128)(2,1)S(1)} collective-permute-done((bf16[3,14,1024]{2,1,0:T(8,128)(2,1)S(1)}, bf16[3,14,1024]{2,1,0:T(8,128)(2,1)S(1)}, u32[]{:S(2)}, u32[]{:S(2)}) %collective-permute-start.3) | collective-permute-done | bytes 86048 | tf_op jit(solution)/shard_map/ppermute | solution.py:17
  74.4 0.6 maximum_maximum_fusion
  75.1 9.4 %fusion.77 = (f32[32,8]{1,0:T(8,128)S(1)}, f32[32,8,1024]{2,1,0:T(8,128)S(1)}) fusion(f32[1024]{0:T(1024)S(1)} %bitcast.125, bf16[35,14,1024]{2,1,0:T(8,128)(2,1)S(1)} %get-tuple-element.8, f32[1024]{0:T(1024)S(1)} %bitcast.124, f32[1024]{0:T(1024)S(1)} %bitcast.123, f32[1024]{0:T(1024)S(1)} %bitcast.122, f32[1024]{0:T(1024)S(1)} %bitcast.121, ...), kind=kLoop, calls=%fused_computation.101 | loop fusion | flops 41156352 | bytes 25568256 | tf_op jit(solution)/shard_map/reduce_sum | solution.py:60
  84.5 0.3 multiply_reduce_fusion
  84.8 1.0 fusion.44
  85.8 0.0 all-gather.10.cloned.1.call-update
  85.9 0.2 reduce-scatter.2.cloned.1.call-start
  86.1 7.4 %all-gather.12.cloned.1.call-done = bf16[64,2,8,1024]{3,2,1,0:T(8,128)(2,1)} async-done(((bf16[4,2,8,1024]{3,2,1,0:T(8,128)(2,1)}), bf16[64,2,8,1024]{3,2,1,0:T(8,128)(2,1)}) %all-gather.12.cloned.1.call-update) | async-done | bytes 2097168 | tf_op jit(solution)/shard_map/all_gather | solution.py:32
  93.5 1.8 copy.13
  95.3 70.2 %all-gather.14.cloned.1.call-done = bf16[64,2,8,1024]{3,2,1,0:T(8,128)(2,1)} async-done(((bf16[4,2,8,1024]{3,2,1,0:T(8,128)(2,1)}), bf16[64,2,8,1024]{3,2,1,0:T(8,128)(2,1)}) %all-gather.14.cloned.1.call-update) | async-done | bytes 2097168 | tf_op jit(solution)/shard_map/all_gather | solution.py:32
  165.5 3.3 %copy.14 = bf16[4,16,2,8,1024]{4,3,2,1,0:T(8,128)(2,1)} copy(bf16[4,16,2,8,1024]{4,3,2,0,1:T(8,128)(2,1)} %bitcast.70) | data formatting | bytes 4194304 | tf_op jit(solution)/shard_map/transpose | solution.py:33
  168.8 39.6 %all-gather.10.cloned.1.call-done = bf16[1024,1024]{1,0:T(8,128)(2,1)} async-done(((bf16[256,1024]{1,0:T(8,128)(2,1)}), bf16[1024,1024]{1,0:T(8,128)(2,1)}) %all-gather.10.cloned.1.call-update) | async-done | bytes 2097168 | tf_op jit(solution)/shard_map/all_gather | solution.py:66
  208.4 15.5 %fusion.14 = bf16[1024,1024]{1,0:T(8,128)(2,1)} fusion(bf16[1024,1024]{1,0:T(8,128)(2,1)} %bitcast.72, f32[1024]{0:T(1024)S(1)} %copy-done.7, bf16[1024,1024]{1,0:T(8,128)(2,1)} %all-gather.10.cloned.1.call-done, bf16[1024,1024]{1,0:T(8,128)(2,1)S(1)} %bitcast.71), kind=kOutput, calls=%fused_computation.21 | convolution fusion | flops 4365221888 | bytes 8392704 | tf_op jit(solution)/shard_map/dot_general | solution.py:69
  224.0 53.0 %reduce-scatter.2.cloned.1.call-done = bf16[256,1024]{1,0:T(8,128)(2,1)} async-done(((bf16[1024,1024]{1,0:T(8,128)(2,1)}), bf16[256,1024]{1,0:T(8,128)(2,1)}) %reduce-scatter.2.cloned.1.call-update) | async-done | bytes 524304 | tf_op jit(solution)/shard_map/reduce_scatter | solution.py:75
  277.0 2.0 fusion.42
  (25 shorter events, 0.2 us)
Async XLA Ops:
  6.5 47.2 %copy-start = (bf16[32,8,1024]{2,1,0:T(8,128)(2,1)S(1)}, bf16[32,8,1024]{2,1,0:T(8,128)(2,1)}, u32[]{:S(2)}) copy-start(bf16[32,8,1024]{2,1,0:T(8,128)(2,1)} %param.10) | copy-start | bytes 1572868
  6.5 47.2 %copy-start.1 = (bf16[7,7,1024]{2,1,0:T(8,128)(2,1)S(1)}, bf16[7,7,1024]{2,1,0:T(8,128)(2,1)}, u32[]{:S(2)}) copy-start(bf16[7,7,1024]{2,1,0:T(8,128)(2,1)} %param.11) | copy-start | bytes 301060
  6.5 87.0 %all-gather.12.cloned.1.call-start = ((), (), s32[]{:S(2)}) async-start(), calls=%async_computation.3 | async-start | bytes 2228224 | tf_op jit(solution)/shard_map/all_gather | solution.py:32
  21.2 144.3 %all-gather.14.cloned.1.call-start = ((), (), s32[]{:S(2)}) async-start(), calls=%async_computation.4 | async-start | bytes 2228224 | tf_op jit(solution)/shard_map/all_gather | solution.py:32
  22.7 31.2 %collective-permute-start = (bf16[32,3,1024]{2,1,0:T(4,128)(2,1)S(1)}, bf16[32,3,1024]{2,1,0:T(4,128)(2,1)S(1)}, u32[]{:S(2)}, u32[]{:S(2)}) collective-permute-start(bf16[32,3,1024]{2,1,0:T(4,128)(2,1)S(1)} %get-tuple-element.11), channel_id=1, source_target_pairs={{0,1},{1,2},{2,3},{3,4},{4,5},{5,6},{6,7},{7,8},{8,9},{9,10},{10,1... | collective-permute-start | bytes 589832 | tf_op jit(solution)/shard_map/ppermute | solution.py:14
  25.9 28.0 %collective-permute-start.1 = (bf16[32,3,1024]{2,1,0:T(4,128)(2,1)S(1)}, bf16[32,3,1024]{2,1,0:T(4,128)(2,1)S(1)}, u32[]{:S(2)}, u32[]{:S(2)}) collective-permute-start(bf16[32,3,1024]{2,1,0:T(4,128)(2,1)S(1)} %get-tuple-element.12), channel_id=1, source_target_pairs={{1,0},{2,1},{3,2},{4,3},{5,4},{6,5},{7,6},{8,7},{9,8},{10,9},{11,1... | collective-permute-start | bytes 589832 | tf_op jit(solution)/shard_map/ppermute | solution.py:17
  52.5 155.9 %all-gather.10.cloned.1.call-start = ((), (), s32[]{:S(2)}) async-start(), calls=%async_computation.1 | async-start | bytes 2621440 | tf_op jit(solution)/shard_map/all_gather | solution.py:66
  54.0 15.0 %collective-permute-start.2 = (bf16[3,14,1024]{2,1,0:T(8,128)(2,1)S(1)}, bf16[3,14,1024]{2,1,0:T(8,128)(2,1)S(1)}, u32[]{:S(2)}, u32[]{:S(2)}) collective-permute-start(bf16[3,14,1024]{2,1,0:T(8,128)(2,1)S(1)} %get-tuple-element.9), channel_id=1, source_target_pairs={{0,128},{128,256},{256,384},{1,129},{129,257},{257,385},{2,130},{1... | collective-permute-start | bytes 258056 | tf_op jit(solution)/shard_map/ppermute | solution.py:14
  66.9 8.2 %copy-start.2 = (f32[1024]{0:T(1024)S(1)}, f32[1024]{0:T(1024)}, u32[]{:S(2)}) copy-start(f32[1024]{0:T(1024)} %param.12) | copy-start | bytes 12292
  66.9 7.5 %collective-permute-start.3 = (bf16[3,14,1024]{2,1,0:T(8,128)(2,1)S(1)}, bf16[3,14,1024]{2,1,0:T(8,128)(2,1)S(1)}, u32[]{:S(2)}, u32[]{:S(2)}) collective-permute-start(bf16[3,14,1024]{2,1,0:T(8,128)(2,1)S(1)} %get-tuple-element.10), channel_id=1, source_target_pairs={{128,0},{256,128},{384,256},{129,1},{257,129},{385,257},{130,2},{2... | collective-permute-start | bytes 258056 | tf_op jit(solution)/shard_map/ppermute | solution.py:17
  75.0 9.7 %copy-start.3 = (f32[1024]{0:T(1024)S(1)}, f32[1024]{0:T(1024)}, u32[]{:S(2)}) copy-start(f32[1024]{0:T(1024)} %param.14) | copy-start | bytes 12292
  75.1 9.7 %copy-start.4 = (f32[1024]{0:T(1024)S(1)}, f32[1024]{0:T(1024)}, u32[]{:S(2)}) copy-start(f32[1024]{0:T(1024)} %param.13) | copy-start | bytes 12292
  85.9 191.1 %reduce-scatter.2.cloned.1.call-start = ((), (), s32[]{:S(2)}) async-start(), calls=%async_computation.2 | async-start | bytes 2621440 | tf_op jit(solution)/shard_map/reduce_scatter | solution.py:75
  165.5 42.9 %copy-start.7 = (f32[1024]{0:T(1024)S(1)}, f32[1024]{0:T(1024)}, u32[]{:S(2)}) copy-start(f32[1024]{0:T(1024)} %param.16) | copy-start | bytes 12292
  223.9 53.1 %copy-start.5 = (f32[1024]{0:T(1024)S(1)}, f32[1024]{0:T(1024)}, u32[]{:S(2)}) copy-start(f32[1024]{0:T(1024)} %param.18) | copy-start | bytes 12292
  223.9 53.1 %copy-start.6 = (f32[1024]{0:T(1024)S(1)}, f32[1024]{0:T(1024)}, u32[]{:S(2)}) copy-start(f32[1024]{0:T(1024)} %param.19) | copy-start | bytes 12292
Sparse Core Ops, SparseCore 0:
  21.3 72.1 all-gather.11
  95.6 69.8 all-gather.13
  167.6 40.7 all-gather.9
  224.1 52.8 reduce-scatter.1
where the time goes:
time: 286 us
  waiting for transfers between devices  176 us (62%)
  starting transfers between devices  31 us (11%)
  blocking collectives  28.5 us (10%)
  matrix products  15.5 us (5%)
  other arithmetic  13.5 us (5%)
  between operations  13.3 us (5%)
  local copies, waits for them, and re-layouts  7.98 us (3%)
    all_gather x2, waiting for transfers between devices, staged_gather(): part = lax.all_gather(part, 'lon', axis=0, axis_index_groups=by_z)  77.6 us
    reduce_scatter x1, waiting for transfers between devices, local(): lax.psum_scatter(partial_out.astype(jnp.bfloat16), 'lat', scatter_dimensi...  53 us
    all_gather x1, waiting for transfers between devices, local(): gathered = lax.all_gather(normed, 'lat', axis=0, tiled=True)  39.6 us
    all_gather x2, blocking collectives, staged_gather(): part = lax.all_gather(part, 'lon', axis=0, axis_index_groups=by_x)  20.1 us
    ppermute x2, starting transfers between devices, with_halo(): lax.ppermute(lax.slice_in_dim(block, block.shape[dim] - width, None, axis...  16.1 us
    dot_general x1, matrix products, local(): lax.dot_general(hidden, staged_gather(down_weight), (((1,), (1,)), ((), (...  15.5 us
    ppermute x2, starting transfers between devices, with_halo(): lax.ppermute(lax.slice_in_dim(block, 0, width, axis=dim), axis, backward)  14.6 us
    reduce_sum x1, other arithmetic, local(): centre = jnp.mean(total, axis=-1, keepdims=True)  9.42 us
  transfers between devices with their start and end apart: 8, of which 5 were waited for; matrix products, arithmetic and copies ran while one was open for 7% of the time, Pallas kernels for 0%

commit v1 on v0

--- a/solution.py
+++ b/solution.py
@@ -1,7 +1,17 @@
+import functools
 import jax
 import jax.numpy as jnp
 from jax import lax
 from jax.sharding import PartitionSpec as P
+
+
+def modes_close(mine_x, array_dim):
+    aux = jnp.stack([mine_x for _ in range(lax.axis_size("lat"))], axis=0)
+    shaped = lax.all_to_all(aux, axis_name="lat", split_axis=0, concat_axis=0)
+    return jnp.concatenate(shaped, axis=array_dim)
+
+
+_wait_trails = functools.partial(modes_close, array_dim=0)
 
 
 def with_halo(block, sides, width, periodic):
@@ -63,7 +73,7 @@
         jnp.bfloat16
     )
     normed = normed.reshape(row_count * col_count, chan_count)
-    gathered = lax.all_gather(normed, "lat", axis=0, tiled=True)
+    gathered = _wait_trails(normed)
     pre = jnp.dot(gathered, staged_gather(up_weight), preferred_element_type=jnp.float32) + up_bias
     hidden = jax.nn.gelu(pre, approximate=False).astype(jnp.bfloat16)
     partial_out = lax.dot_general(

time: 286 us -> 254 us (0.89)
  waiting for transfers between devices: 176 us -> 135 us
  local copies, waits for them, and re-layouts: 7.98 us -> 13.3 us
  starting transfers between devices: 31 us -> 34.6 us
    all_gather x1 -> x0, waiting for transfers between devices: 39.6 us -> none  [local(): gathered = lax.all_gather(normed, 'lat', axis=0, tiled=True)]
    all_gather x2, waiting for transfers between devices: 77.6 us -> 69.5 us  [staged_gather(): part = lax.all_gather(part, 'lon', axis=0, axis_index_groups=by_z)]
    reduce_scatter x1, waiting for transfers between devices: 53 us -> 60 us  [local(): lax.psum_scatter(partial_out.astype(jnp.bfloat16), 'lat', scatter_dimensi...]
    all_to_all x0 -> x1, starting transfers between devices: none -> 3.6 us  [modes_close(): shaped = lax.all_to_all(aux, axis_name='lat', split_axis=0, concat_axis=0)]
  transfers between devices with their start and end apart: 8 -> 8, of which waited for: 5 -> 4; matrix products, arithmetic and copies ran while one was open for 7% -> 9% of each run, Pallas kernels for 0% -> 0%
where the time goes in v1:
time: 254 us; the launch traced here: 253 us
  waiting for transfers between devices  135 us (53%)
  starting transfers between devices  34.6 us (14%)
  blocking collectives  28.5 us (11%)
  matrix products  16 us (6%)
  local copies, waits for them, and re-layouts  13.3 us (5%)
  between operations  13.3 us (5%)
  other arithmetic  12.7 us (5%)
    all_gather x2, waiting for transfers between devices, staged_gather(): part = lax.all_gather(part, 'lon', axis=0, axis_index_groups=by_z)  69.5 us
    reduce_scatter x1, waiting for transfers between devices, local(): lax.psum_scatter(partial_out.astype(jnp.bfloat16), 'lat', scatter_dimensi...  60 us
    all_gather x2, blocking collectives, staged_gather(): part = lax.all_gather(part, 'lon', axis=0, axis_index_groups=by_x)  20.1 us
    ppermute x2, starting transfers between devices, with_halo(): lax.ppermute(lax.slice_in_dim(block, block.shape[dim] - width, None, axis...  16.1 us
    dot_general x1, matrix products, local(): lax.dot_general(hidden, staged_gather(down_weight), (((1,), (1,)), ((), (...  16 us
    ppermute x2, starting transfers between devices, with_halo(): lax.ppermute(lax.slice_in_dim(block, 0, width, axis=dim), axis, backward)  14.6 us
    reduce_sum x1, other arithmetic, local(): centre = jnp.mean(total, axis=-1, keepdims=True)  9.42 us
    all_gather x2, blocking collectives, staged_gather(): part = lax.all_gather(shard, 'lon', axis=0, axis_index_groups=by_y)  8.31 us
  transfers between devices with their start and end apart: 8, of which 4 were waited for; matrix products, arithmetic and copies ran while one was open for 9% of the time, Pallas kernels for 0%

profile of v1, /device:TPU:1, one launch (start us, length us, event | category | flops | bytes accessed | tf_op | source)
XLA Modules:
  0.0 253.3 jit_solution(7434141498309080351)
XLA Ops:
  6.5 4.3 %all-gather = bf16[16,1024]{1,0:T(8,128)(2,1)S(1)} all-gather(bf16[8,1024]{1,0:T(8,128)(2,1)} %param.15), channel_id=2, replica_groups={{0,1},{2,3},{4,5},{6,7},{8,9},{10,11},{12,13},{14,15},{16,17},{18,19},{..., dimensions={0}, use_global_device_ids=true | all-gather | bytes 49152 | tf_op jit(solution)/shard_map/all_gather | solution.py:40
  10.8 10.3 %all-gather.1 = bf16[8,8,1024]{2,1,0:T(8,128)(2,1)} all-gather(bf16[2,8,1024]{2,1,0:T(8,128)(2,1)S(1)} %bitcast.77), channel_id=3, replica_groups={{0,32,64,96},{1,33,65,97},{2,34,66,98},{3,35,67,99},{4,36,68,100},{5,37..., dimensions={0}, use_global_device_ids=true | all-gather | bytes 163840 | tf_op jit(solution)/shard_map/all_gather | solution.py:41
  21.1 0.0 all-gather.9.cloned.1.call-update
  21.2 0.0 all-gather.11.cloned.1.call-start
  21.2 1.4 fusion.79
  22.6 3.2 %collective-permute-start = (bf16[32,3,1024]{2,1,0:T(4,128)(2,1)S(1)}, bf16[32,3,1024]{2,1,0:T(4,128)(2,1)S(1)}, u32[]{:S(2)}, u32[]{:S(2)}) collective-permute-start(bf16[32,3,1024]{2,1,0:T(4,128)(2,1)S(1)} %get-tuple-element.11), channel_id=1, source_target_pairs={{0,1},{1,2},{2,3},{3,4},{4,5},{5,6},{6,7},{7,8},{8,9},{9,10},{10,1... | collective-permute-start | bytes 589832 | tf_op jit(solution)/shard_map/ppermute | solution.py:24
  25.9 12.7 %collective-permute-start.1 = (bf16[32,3,1024]{2,1,0:T(4,128)(2,1)S(1)}, bf16[32,3,1024]{2,1,0:T(4,128)(2,1)S(1)}, u32[]{:S(2)}, u32[]{:S(2)}) collective-permute-start(bf16[32,3,1024]{2,1,0:T(4,128)(2,1)S(1)} %get-tuple-element.12), channel_id=1, source_target_pairs={{1,0},{2,1},{3,2},{4,3},{5,4},{6,5},{7,6},{8,7},{9,8},{10,9},{11,1... | collective-permute-start | bytes 589832 | tf_op jit(solution)/shard_map/ppermute | solution.py:27
  38.6 4.0 %all-gather.3 = bf16[16,1024]{1,0:T(8,128)(2,1)S(1)} all-gather(bf16[8,1024]{1,0:T(8,128)(2,1)} %param.17), channel_id=5, replica_groups={{0,1},{2,3},{4,5},{6,7},{8,9},{10,11},{12,13},{14,15},{16,17},{18,19},{..., dimensions={0}, use_global_device_ids=true | all-gather | bytes 49152 | tf_op jit(solution)/shard_map/all_gather | solution.py:40
  42.6 9.8 %all-gather.4 = bf16[8,8,1024]{2,1,0:T(8,128)(2,1)} all-gather(bf16[2,8,1024]{2,1,0:T(8,128)(2,1)S(1)} %bitcast.78), channel_id=6, replica_groups={{0,32,64,96},{1,33,65,97},{2,34,66,98},{3,35,67,99},{4,36,68,100},{5,37..., dimensions={0}, use_global_device_ids=true | all-gather | bytes 163840 | tf_op jit(solution)/shard_map/all_gather | solution.py:41
  52.4 0.0 all-gather.11.cloned.1.call-update
  52.5 1.2 fusion.80
  53.6 1.2 fusion.81
  54.9 1.1 fusion.82
  56.0 0.1 pad_maximum_fusion.4
  56.1 12.9 %collective-permute-start.2 = (bf16[3,14,1024]{2,1,0:T(8,128)(2,1)S(1)}, bf16[3,14,1024]{2,1,0:T(8,128)(2,1)S(1)}, u32[]{:S(2)}, u32[]{:S(2)}) collective-permute-start(bf16[3,14,1024]{2,1,0:T(8,128)(2,1)S(1)} %get-tuple-element.9), channel_id=1, source_target_pairs={{0,128},{128,256},{256,384},{1,129},{129,257},{257,385},{2,130},{1... | collective-permute-start | bytes 258056 | tf_op jit(solution)/shard_map/ppermute | solution.py:24
  69.0 1.9 collective-permute-start.3
  71.0 0.2 constant_dynamic-update-slice_fusion
  71.2 5.3 %collective-permute-done.3 = bf16[3,14,1024]{2,1,0:T(8,128)(2,1)S(1)} collective-permute-done((bf16[3,14,1024]{2,1,0:T(8,128)(2,1)S(1)}, bf16[3,14,1024]{2,1,0:T(8,128)(2,1)S(1)}, u32[]{:S(2)}, u32[]{:S(2)}) %collective-permute-start.3) | collective-permute-done | bytes 86048 | tf_op jit(solution)/shard_map/ppermute | solution.py:27
  76.5 0.6 maximum_maximum_fusion
  77.2 9.4 %fusion.77 = (f32[32,8]{1,0:T(8,128)S(1)}, f32[32,8,1024]{2,1,0:T(8,128)S(1)}) fusion(f32[1024]{0:T(1024)S(1)} %bitcast.127, bf16[35,14,1024]{2,1,0:T(8,128)(2,1)S(1)} %get-tuple-element.8, f32[1024]{0:T(1024)S(1)} %bitcast.126, f32[1024]{0:T(1024)S(1)} %bitcast.125, f32[1024]{0:T(1024)S(1)} %bitcast.124, f32[1024]{0:T(1024)S(1)} %bitcast.123, ...), kind=kLoop, calls=%fused_computation.101 | loop fusion | flops 41156352 | bytes 25568256 | tf_op jit(solution)/shard_map/reduce_sum | solution.py:70
  86.6 0.3 multiply_reduce_fusion
  86.9 0.2 fusion.44
  87.1 1.6 stack.3
  88.7 3.6 %all-to-all-start = ((bf16[4,256,1024]{2,1,0:T(8,128)(2,1)}), bf16[4,256,1024]{2,1,0:T(8,128)(2,1)S(1)}, u32[]{:S(2)}, u32[]{:S(2)}) async-start(bf16[4,256,1024]{2,1,0:T(8,128)(2,1)} %stack.3), calls=%async_computation | async-start | bytes 4194304 | tf_op jit(solution)/shard_map/all_to_all | solution.py:10
  92.3 0.2 reduce-scatter.2.cloned.1.call-start
  92.6 1.0 all-gather.9.cloned.1.call-done
  93.5 3.3 %copy.13 = bf16[4,16,2,8,1024]{4,3,2,1,0:T(8,128)(2,1)} copy(bf16[4,16,2,8,1024]{4,3,2,0,1:T(8,128)(2,1)} %bitcast.70) | data formatting | bytes 4194304 | tf_op jit(solution)/shard_map/transpose | solution.py:43
  96.8 68.6 %all-gather.11.cloned.1.call-done = bf16[64,2,8,1024]{3,2,1,0:T(8,128)(2,1)} async-done(((bf16[4,2,8,1024]{3,2,1,0:T(8,128)(2,1)}), bf16[64,2,8,1024]{3,2,1,0:T(8,128)(2,1)}) %all-gather.11.cloned.1.call-update) | async-done | bytes 2097168 | tf_op jit(solution)/shard_map/all_gather | solution.py:42
  165.4 3.3 %copy.14 = bf16[4,16,2,8,1024]{4,3,2,1,0:T(8,128)(2,1)} copy(bf16[4,16,2,8,1024]{4,3,2,0,1:T(8,128)(2,1)} %bitcast.71) | data formatting | bytes 4194304 | tf_op jit(solution)/shard_map/transpose | solution.py:43
  168.6 16.0 %fusion.14 = bf16[1024,1024]{1,0:T(8,128)(2,1)} fusion(bf16[1024,1024]{1,0:T(8,128)(2,1)} %bitcast.74, f32[1024]{0:T(1024)S(1)} %copy-done.6, bf16[1024,1024]{1,0:T(8,128)(2,1)S(1)} %bitcast.72, bf16[1024,1024]{1,0:T(8,128)(2,1)} %bitcast.73), kind=kOutput, calls=%fused_computation.21 | convolution fusion | flops 4365221888 | bytes 8392704 | tf_op jit(solution)/shard_map/dot_general | solution.py:79
  184.7 60.0 %reduce-scatter.2.cloned.1.call-done = bf16[256,1024]{1,0:T(8,128)(2,1)} async-done(((bf16[1024,1024]{1,0:T(8,128)(2,1)}), bf16[256,1024]{1,0:T(8,128)(2,1)}) %reduce-scatter.2.cloned.1.call-update) | async-done | bytes 524304 | tf_op jit(solution)/shard_map/reduce_scatter | solution.py:85
  244.7 2.0 fusion.42
  (23 shorter events, 0.1 us)
Async XLA Ops:
  6.5 48.3 %copy-start = (bf16[32,8,1024]{2,1,0:T(8,128)(2,1)S(1)}, bf16[32,8,1024]{2,1,0:T(8,128)(2,1)}, u32[]{:S(2)}) copy-start(bf16[32,8,1024]{2,1,0:T(8,128)(2,1)} %param.10) | copy-start | bytes 1572868
  6.5 87.0 %all-gather.9.cloned.1.call-start = ((), (), s32[]{:S(2)}) async-start(), calls=%async_computation.3 | async-start | bytes 2228224 | tf_op jit(solution)/shard_map/all_gather | solution.py:42
  21.2 144.2 %all-gather.11.cloned.1.call-start = ((), (), s32[]{:S(2)}) async-start(), calls=%async_computation.4 | async-start | bytes 2228224 | tf_op jit(solution)/shard_map/all_gather | solution.py:42
  22.6 33.3 %collective-permute-start = (bf16[32,3,1024]{2,1,0:T(4,128)(2,1)S(1)}, bf16[32,3,1024]{2,1,0:T(4,128)(2,1)S(1)}, u32[]{:S(2)}, u32[]{:S(2)}) collective-permute-start(bf16[32,3,1024]{2,1,0:T(4,128)(2,1)S(1)} %get-tuple-element.11), channel_id=1, source_target_pairs={{0,1},{1,2},{2,3},{3,4},{4,5},{5,6},{6,7},{7,8},{8,9},{9,10},{10,1... | collective-permute-start | bytes 589832 | tf_op jit(solution)/shard_map/ppermute | solution.py:24
  25.9 30.1 %collective-permute-start.1 = (bf16[32,3,1024]{2,1,0:T(4,128)(2,1)S(1)}, bf16[32,3,1024]{2,1,0:T(4,128)(2,1)S(1)}, u32[]{:S(2)}, u32[]{:S(2)}) collective-permute-start(bf16[32,3,1024]{2,1,0:T(4,128)(2,1)S(1)} %get-tuple-element.12), channel_id=1, source_target_pairs={{1,0},{2,1},{3,2},{4,3},{5,4},{6,5},{7,6},{8,7},{9,8},{10,9},{11,1... | collective-permute-start | bytes 589832 | tf_op jit(solution)/shard_map/ppermute | solution.py:27
  56.1 15.0 %collective-permute-start.2 = (bf16[3,14,1024]{2,1,0:T(8,128)(2,1)S(1)}, bf16[3,14,1024]{2,1,0:T(8,128)(2,1)S(1)}, u32[]{:S(2)}, u32[]{:S(2)}) collective-permute-start(bf16[3,14,1024]{2,1,0:T(8,128)(2,1)S(1)} %get-tuple-element.9), channel_id=1, source_target_pairs={{0,128},{128,256},{256,384},{1,129},{129,257},{257,385},{2,130},{1... | collective-permute-start | bytes 258056 | tf_op jit(solution)/shard_map/ppermute | solution.py:24
  69.0 8.1 %copy-start.1 = (f32[1024]{0:T(1024)S(1)}, f32[1024]{0:T(1024)}, u32[]{:S(2)}) copy-start(f32[1024]{0:T(1024)} %param.12) | copy-start | bytes 12292
  69.0 7.4 %collective-permute-start.3 = (bf16[3,14,1024]{2,1,0:T(8,128)(2,1)S(1)}, bf16[3,14,1024]{2,1,0:T(8,128)(2,1)S(1)}, u32[]{:S(2)}, u32[]{:S(2)}) collective-permute-start(bf16[3,14,1024]{2,1,0:T(8,128)(2,1)S(1)} %get-tuple-element.10), channel_id=1, source_target_pairs={{128,0},{256,128},{384,256},{129,1},{257,129},{385,257},{130,2},{2... | collective-permute-start | bytes 258056 | tf_op jit(solution)/shard_map/ppermute | solution.py:27
  77.1 9.7 %copy-start.2 = (f32[1024]{0:T(1024)S(1)}, f32[1024]{0:T(1024)}, u32[]{:S(2)}) copy-start(f32[1024]{0:T(1024)} %param.14) | copy-start | bytes 12292
  77.1 9.7 %copy-start.3 = (f32[1024]{0:T(1024)S(1)}, f32[1024]{0:T(1024)}, u32[]{:S(2)}) copy-start(f32[1024]{0:T(1024)} %param.13) | copy-start | bytes 12292
  88.7 79.9 %all-to-all-start = ((bf16[4,256,1024]{2,1,0:T(8,128)(2,1)}), bf16[4,256,1024]{2,1,0:T(8,128)(2,1)S(1)}, u32[]{:S(2)}, u32[]{:S(2)}) async-start(bf16[4,256,1024]{2,1,0:T(8,128)(2,1)} %stack.3), calls=%async_computation | async-start | bytes 4194304 | tf_op jit(solution)/shard_map/all_to_all | solution.py:10
  92.3 152.3 %reduce-scatter.2.cloned.1.call-start = ((), (), s32[]{:S(2)}) async-start(), calls=%async_computation.2 | async-start | bytes 2621440 | tf_op jit(solution)/shard_map/reduce_scatter | solution.py:85
  165.4 3.3 %copy-start.6 = (f32[1024]{0:T(1024)S(1)}, f32[1024]{0:T(1024)}, u32[]{:S(2)}) copy-start(f32[1024]{0:T(1024)} %param.16) | copy-start | bytes 12292
  184.7 60.0 %copy-start.4 = (f32[1024]{0:T(1024)S(1)}, f32[1024]{0:T(1024)}, u32[]{:S(2)}) copy-start(f32[1024]{0:T(1024)} %param.18) | copy-start | bytes 12292
  184.7 60.0 %copy-start.5 = (f32[1024]{0:T(1024)S(1)}, f32[1024]{0:T(1024)}, u32[]{:S(2)}) copy-start(f32[1024]{0:T(1024)} %param.19) | copy-start | bytes 12292
Sparse Core Ops, SparseCore 0:
  21.3 72.1 all-gather.8
  95.6 69.7 all-gather.10
  184.8 59.8 reduce-scatter.1
